TPU v7x, 32 devices: a whole 2x2x4 slice. The times are simulated.
32 devices in a mesh: gy: 8 (over y, x, core), gz: 4 (over z).
Axes of the slice: x: 2, y: 2, z: 4, core: 2. Of those that a mesh axis runs over, the one named last changes fastest.
Arguments:
- pressure_cotangent: bfloat16 [32, 1024, 2048], P('gz', 'gy'), may hold values from -6 to 6
- velocity_cotangent: bfloat16 [32, 1024, 2048], P('gz', 'gy'), may hold values from -6 to 6
- inverse_spacing: float32 [32], P('gz'), may hold values from 0.5 to 4
- inverse_pivot: float32 [32, 2048, 1024], P('gz', 'gy'), may hold values from 0.02 to 0.1
- lower_factor: float32 [32, 2048, 1024], P('gz', 'gy'), may hold values from 0.04 to 0.998, as said below
- upper_factor: float32 [32, 2048, 1024], P('gz', 'gy'), may hold values from 0.04 to 0.998, as said below
Outputs:
- pressure_adjoint: bfloat16 [32, 1024, 2048], P('gz', 'gy')
Inputs may be any that keep to these rules, and one draw needn't show every extreme that they name: `lower_factor`: multiplier carried from one level to the next. `upper_factor`: multiplier carried from one level to the next.
All inputs are finite; a program needn't handle non-finite values.
Results may differ from a plain program's by a relative error of at most 0.0018.
Values may be sent and summed in bfloat16 or wider, within the bound.
A program may use at most 192 MiB of HBM per device.

v0:
```python
import math

import jax
import jax.numpy as jnp
from jax import lax
from jax.sharding import PartitionSpec as P

TWIDDLE_PRECISION = lax.Precision.HIGH


def passed_along(x, axis, by):
    size = lax.axis_size(axis)
    pairs = [(i, i + by) for i in range(size) if 0 <= i + by < size]
    return lax.ppermute(x, axis, pairs)


def entering(part, axis, combine, identity, reverse):
    count = lax.axis_size(axis)
    place = lax.axis_index(axis)
    ahead = count - 1 - place if reverse else place
    gathered = jax.tree.map(lambda a: lax.all_gather(a, axis), part)
    state = jax.tree.map(lambda a, e: jnp.zeros_like(a) + jnp.asarray(e, a.dtype), part, identity)

    def one(turn, state):
        source = count - 1 - turn if reverse else turn
        return combine(
            state, jax.tree.map(lambda a: lax.dynamic_index_in_dim(a, source, 0, False), gathered)
        )

    return lax.fori_loop(0, ahead, one, state)


def angle_parts(x_cells, block_half, column_start, tile_width):
    column = column_start + lax.broadcasted_iota(jnp.int32, (x_cells, tile_width), 1)
    sample = lax.broadcasted_iota(jnp.int32, (x_cells, tile_width), 0)
    block_index = column // (2 * block_half)
    within = column % (2 * block_half)
    wavenumber = block_index * block_half + within % block_half
    phase_index = sample * wavenumber % x_cells
    angle_value = phase_index.astype(jnp.float32) * (2.0 * math.pi / x_cells)
    return jnp.where(within < block_half, jnp.cos(angle_value), -jnp.sin(angle_value))


def to_spectrum(source, block_half):
    level_heights, row_count, x_cells = source.shape
    tile_width = min(512, 2 * x_cells)
    tile_count = 2 * x_cells // tile_width

    def advance(tile_index, spectrum):
        twiddle = angle_parts(x_cells, block_half, tile_index * tile_width, tile_width)
        product = jnp.einsum("zyn,nc->zyc", source, twiddle, precision=TWIDDLE_PRECISION)
        return lax.dynamic_update_slice_in_dim(spectrum, product, tile_index * tile_width, 2)

    initial = jnp.zeros((level_heights, row_count, 2 * x_cells), jnp.float32)
    return lax.fori_loop(0, tile_count, advance, initial)


def to_field(spectrum, block_half, normalizer):
    level_heights, row_count, doubled = spectrum.shape
    x_cells = doubled // 2
    tile_width = min(512, doubled)
    tile_count = doubled // tile_width

    def advance(tile_index, pressure_field):
        twiddle = angle_parts(x_cells, block_half, tile_index * tile_width, tile_width)
        column_piece = lax.dynamic_slice_in_dim(spectrum, tile_index * tile_width, tile_width, 2)
        return pressure_field + jnp.einsum(
            "zyc,nc->zyn", column_piece, twiddle, precision=TWIDDLE_PRECISION
        )

    initial = jnp.zeros((level_heights, row_count, x_cells), jnp.float32)
    return lax.fori_loop(0, tile_count, advance, initial) * normalizer


def wave_tables(count):
    row_index = lax.broadcasted_iota(jnp.int32, (count, count), 0)
    col_index = lax.broadcasted_iota(jnp.int32, (count, count), 1)
    phase_index = row_index * col_index % count
    angle_value = phase_index.astype(jnp.float32) * (2.0 * math.pi / count)
    return (jnp.cos(angle_value), jnp.sin(angle_value))


def along_span(stacked, block_half, cosine, sine):
    cosine_part = jnp.einsum("ky,zyc->zck", cosine, stacked, precision=TWIDDLE_PRECISION)
    sine_part = jnp.einsum("ky,zyc->zck", sine, stacked, precision=TWIDDLE_PRECISION)
    cosine_component = cosine_part[:, :block_half] + sine_part[:, block_half:]
    imag_part = cosine_part[:, block_half:] - sine_part[:, :block_half]
    return (cosine_component, imag_part)


def back_span(cosine_component, imag_part, block_half, cosine, sine):
    stacked = jnp.concatenate([cosine_component, imag_part], axis=1)
    cosine_part = jnp.einsum("ky,zck->zyc", cosine, stacked, precision=TWIDDLE_PRECISION)
    sine_part = jnp.einsum("ky,zck->zyc", sine, stacked, precision=TWIDDLE_PRECISION)
    real_out = cosine_part[..., :block_half] - sine_part[..., block_half:]
    imag_out = cosine_part[..., block_half:] + sine_part[..., :block_half]
    return jnp.concatenate([real_out, imag_out], axis=2)


def sweep_down(cosine_component, imag_part, diagonal_divisors, lowers):

    def advance(running, layer_values):
        run_real, run_imag, gain_chain = running
        force_real, force_imag, pivot_values, lower_values = layer_values
        run_real = pivot_values * force_real + lower_values * run_real
        run_imag = pivot_values * force_imag + lower_values * run_imag
        gain_chain = lower_values * gain_chain
        return ((run_real, run_imag, gain_chain), (run_real, run_imag, gain_chain))

    empty_field = jnp.zeros_like(cosine_component[0])
    start_state = (empty_field, empty_field, jnp.ones_like(empty_field))
    _, outputs = lax.scan(
        advance, start_state, (cosine_component, imag_part, diagonal_divisors, lowers)
    )
    return outputs


def sweep_up(cosine_component, imag_part, uppers):

    def advance(running, layer_values):
        run_real, run_imag, gain_chain = running
        force_real, force_imag, upper_values = layer_values
        run_real = force_real + upper_values * run_real
        run_imag = force_imag + upper_values * run_imag
        gain_chain = upper_values * gain_chain
        return ((run_real, run_imag, gain_chain), (run_real, run_imag, gain_chain))

    empty_field = jnp.zeros_like(cosine_component[0])
    start_state = (empty_field, empty_field, jnp.ones_like(empty_field))
    _, outputs = lax.scan(advance, start_state, (cosine_component, imag_part, uppers), reverse=True)
    return outputs


def compose(earlier, later):
    gain_early, real_early, imag_early = earlier
    gain_late, cosine_component_final, imag_late = later
    return (
        gain_late * gain_early,
        gain_late * real_early + cosine_component_final,
        gain_late * imag_early + imag_late,
    )


def on_device(
    pressure_cotangent,
    velocity_cotangent,
    inverse_spacing,
    inverse_pivot,
    lower_factor,
    upper_factor,
):
    level_heights, row_count, x_cells = pressure_cotangent.shape
    level_above = passed_along(velocity_cotangent[:1], "gz", -1)
    velocity = velocity_cotangent.astype(jnp.float32)
    shifted = jnp.concatenate([velocity[1:], level_above.astype(jnp.float32)], 0)
    source = pressure_cotangent.astype(jnp.float32) + inverse_spacing[:, None, None] * (
        shifted - velocity
    )
    span_count = lax.axis_size("gy")
    span_total = row_count * span_count
    cosine, sine = wave_tables(span_total)
    normalizer = 1.0 / (x_cells * span_total)
    block_half = x_cells // span_count
    spectrum = to_spectrum(source, block_half).reshape(
        level_heights, row_count, span_count, 2 * block_half
    )
    arrived = lax.all_to_all(spectrum, "gy", split_axis=2, concat_axis=1, tiled=True)
    arrived = arrived.reshape(level_heights, span_total, 2 * block_half)
    cosine_component, imag_part = along_span(arrived, block_half, cosine, sine)
    down_real, down_imag, down_gain = sweep_down(
        cosine_component, imag_part, inverse_pivot, lower_factor
    )
    empty_field = jnp.zeros_like(down_gain[0])
    identity = (jnp.ones_like(empty_field), empty_field, empty_field)
    summary_down = (down_gain[-1], down_real[-1], down_imag[-1])
    _, enter_real, enter_imag = entering(summary_down, "gz", compose, identity, False)
    low_real = down_real + down_gain * enter_real
    low_imag = down_imag + down_gain * enter_imag
    up_real, up_imag, up_gain = sweep_up(low_real, low_imag, upper_factor)
    summary_up = (up_gain[0], up_real[0], up_imag[0])
    _, above_real, above_imag = entering(summary_up, "gz", compose, identity, True)
    solved_real = up_real + up_gain * above_real
    solved_imag = up_imag + up_gain * above_imag
    stacked = back_span(solved_real, solved_imag, block_half, cosine, sine)
    stacked = stacked.reshape(level_heights, span_total, 1, 2 * block_half)
    returned = lax.all_to_all(stacked, "gy", split_axis=1, concat_axis=2, tiled=True)
    spectrum_back = returned.reshape(level_heights, row_count, 2 * x_cells)
    pressure_field = to_field(spectrum_back, block_half, normalizer)
    return pressure_field.astype(jnp.bfloat16)


def solution(mesh):
    in_specs = (
        P("gz", "gy", None),
        P("gz", "gy", None),
        P("gz"),
        P("gz", "gy", None),
        P("gz", "gy", None),
        P("gz", "gy", None),
    )
    out_specs = P("gz", "gy", None)
    return jax.shard_map(
        on_device, mesh=mesh, in_specs=in_specs, out_specs=out_specs, check_vma=False
    )
```

profile of v0, /device:TPU:0, one launch (start us, length us, event | category | flops | bytes accessed | tf_op | source)
XLA Modules:
  0.0 1925.2 jit_solution(17286963578909093910)
XLA Ops:
  40.5 295.4 %while.109 = (s32[]{:T(128)}, f32[8,128,4096]{1,2,0:T(8,128)}, f32[8,128,2048]{2,1,0:T(8,128)}, s32[]{:T(128)}, s32[]{:T(128)}, /*index=5*/s32[]{:T(128)}, s32[]{:T(128)}) while((s32[]{:T(128)}, f32[8,128,4096]{1,2,0:T(8,128)}, f32[8,128,2048]{2,1,0:T(8,128)}, s32[]{:T(128)}, s32[]{:T(128)}, /*index=5*/s32[]{:T(128)}, s32[]{:T(128)}) %tuple.215), condition=%wide.region_1.2_spmd, body=%wide.region_0.1_spmd.sunk | while | flops 6476023296 | bytes 10504331 | solution.py:55
  40.5 36.9 %bitcast_dynamic-update-slice_fusion.10 = f32[8,128,4096]{1,2,0:T(8,128)} fusion(f32[8,128,4096]{1,2,0:T(8,128)} %get-tuple-element.1207, s32[]{:T(128)S(6)} %select_n.392, f32[8,128,2048]{2,1,0:T(8,128)} %get-tuple-element.1215, s32[512]{0:T(512)S(1)} %get-tuple-element.1133, s32[512]{0:T(512)S(1)} %get-tuple-element.1134, ...), kind=kOutput, calls=%fused_computation.27.clone.2 | convolution fusion | flops 6476005376 | bytes 10494980 | tf_op jit(solution)/shard_map/while/body/eval_jaxpr/zyn,nc->zyc/dot_general | solution.py:51
  77.4 36.9 %bitcast_dynamic-update-slice_fusion.10 = f32[8,128,4096]{1,2,0:T(8,128)} fusion(f32[8,128,4096]{1,2,0:T(8,128)} %get-tuple-element.1207, s32[]{:T(128)S(6)} %select_n.392, f32[8,128,2048]{2,1,0:T(8,128)} %get-tuple-element.1215, s32[512]{0:T(512)S(1)} %get-tuple-element.1133, s32[512]{0:T(512)S(1)} %get-tuple-element.1134, ...), kind=kOutput, calls=%fused_computation.27.clone.2 | convolution fusion | flops 6476005376 | bytes 10494980 | tf_op jit(solution)/shard_map/while/body/eval_jaxpr/zyn,nc->zyc/dot_general | solution.py:51
  114.4 36.9 %bitcast_dynamic-update-slice_fusion.10 = f32[8,128,4096]{1,2,0:T(8,128)} fusion(f32[8,128,4096]{1,2,0:T(8,128)} %get-tuple-element.1207, s32[]{:T(128)S(6)} %select_n.392, f32[8,128,2048]{2,1,0:T(8,128)} %get-tuple-element.1215, s32[512]{0:T(512)S(1)} %get-tuple-element.1133, s32[512]{0:T(512)S(1)} %get-tuple-element.1134, ...), kind=kOutput, calls=%fused_computation.27.clone.2 | convolution fusion | flops 6476005376 | bytes 10494980 | tf_op jit(solution)/shard_map/while/body/eval_jaxpr/zyn,nc->zyc/dot_general | solution.py:51
  151.3 36.9 %bitcast_dynamic-update-slice_fusion.10 = f32[8,128,4096]{1,2,0:T(8,128)} fusion(f32[8,128,4096]{1,2,0:T(8,128)} %get-tuple-element.1207, s32[]{:T(128)S(6)} %select_n.392, f32[8,128,2048]{2,1,0:T(8,128)} %get-tuple-element.1215, s32[512]{0:T(512)S(1)} %get-tuple-element.1133, s32[512]{0:T(512)S(1)} %get-tuple-element.1134, ...), kind=kOutput, calls=%fused_computation.27.clone.2 | convolution fusion | flops 6476005376 | bytes 10494980 | tf_op jit(solution)/shard_map/while/body/eval_jaxpr/zyn,nc->zyc/dot_general | solution.py:51
  188.2 36.9 %bitcast_dynamic-update-slice_fusion.10 = f32[8,128,4096]{1,2,0:T(8,128)} fusion(f32[8,128,4096]{1,2,0:T(8,128)} %get-tuple-element.1207, s32[]{:T(128)S(6)} %select_n.392, f32[8,128,2048]{2,1,0:T(8,128)} %get-tuple-element.1215, s32[512]{0:T(512)S(1)} %get-tuple-element.1133, s32[512]{0:T(512)S(1)} %get-tuple-element.1134, ...), kind=kOutput, calls=%fused_computation.27.clone.2 | convolution fusion | flops 6476005376 | bytes 10494980 | tf_op jit(solution)/shard_map/while/body/eval_jaxpr/zyn,nc->zyc/dot_general | solution.py:51
  225.2 36.9 %bitcast_dynamic-update-slice_fusion.10 = f32[8,128,4096]{1,2,0:T(8,128)} fusion(f32[8,128,4096]{1,2,0:T(8,128)} %get-tuple-element.1207, s32[]{:T(128)S(6)} %select_n.392, f32[8,128,2048]{2,1,0:T(8,128)} %get-tuple-element.1215, s32[512]{0:T(512)S(1)} %get-tuple-element.1133, s32[512]{0:T(512)S(1)} %get-tuple-element.1134, ...), kind=kOutput, calls=%fused_computation.27.clone.2 | convolution fusion | flops 6476005376 | bytes 10494980 | tf_op jit(solution)/shard_map/while/body/eval_jaxpr/zyn,nc->zyc/dot_general | solution.py:51
  262.1 36.9 %bitcast_dynamic-update-slice_fusion.10 = f32[8,128,4096]{1,2,0:T(8,128)} fusion(f32[8,128,4096]{1,2,0:T(8,128)} %get-tuple-element.1207, s32[]{:T(128)S(6)} %select_n.392, f32[8,128,2048]{2,1,0:T(8,128)} %get-tuple-element.1215, s32[512]{0:T(512)S(1)} %get-tuple-element.1133, s32[512]{0:T(512)S(1)} %get-tuple-element.1134, ...), kind=kOutput, calls=%fused_computation.27.clone.2 | convolution fusion | flops 6476005376 | bytes 10494980 | tf_op jit(solution)/shard_map/while/body/eval_jaxpr/zyn,nc->zyc/dot_general | solution.py:51
  299.0 36.9 %bitcast_dynamic-update-slice_fusion.10 = f32[8,128,4096]{1,2,0:T(8,128)} fusion(f32[8,128,4096]{1,2,0:T(8,128)} %get-tuple-element.1207, s32[]{:T(128)S(6)} %select_n.392, f32[8,128,2048]{2,1,0:T(8,128)} %get-tuple-element.1215, s32[512]{0:T(512)S(1)} %get-tuple-element.1133, s32[512]{0:T(512)S(1)} %get-tuple-element.1134, ...), kind=kOutput, calls=%fused_computation.27.clone.2 | convolution fusion | flops 6476005376 | bytes 10494980 | tf_op jit(solution)/shard_map/while/body/eval_jaxpr/zyn,nc->zyc/dot_general | solution.py:51
  386.0 151.2 %all-to-all-done = f32[8,128,8,512]{1,3,0,2:T(8,128)} async-done(((f32[8,128,8,512]{1,3,0,2:T(8,128)}), f32[8,128,8,512]{1,3,0,2:T(8,128)}, u32[]{:S(2)}, u32[]{:S(2)}) %all-to-all-start) | async-done | bytes 16777248 | tf_op jit(solution)/shard_map/all_to_all | solution.py:167
  572.9 32.5 %fusion.95 = f32[8,512,1024]{2,1,0:T(8,128)} fusion(f32[8,1024,512]{1,2,0:T(8,128)} %reshape.22, f32[1024,1024,1]{1,0,2:T(8,128)} %fusion.149), kind=kOutput, calls=%fused_computation.164 | convolution fusion | flops 25769803776 | bytes 37748736 | tf_op jit(solution)/shard_map/ky,zyc->zck/dot_general | solution.py:85
  605.4 29.2 %fusion.98 = f32[8,512,1024]{2,1,0:T(8,128)} fusion(f32[8,1024,512]{1,2,0:T(8,128)S(1)} %copy-done.3, f32[1024,1024,1]{1,0,2:T(8,128)S(1)} %copy-done.4), kind=kOutput, calls=%fused_computation.167 | convolution fusion | flops 25769803776 | bytes 37748736 | tf_op jit(solution)/shard_map/ky,zyc->zck/dot_general | solution.py:84
  666.3 41.1 %while.112 = (s32[]{:T(128)}, f32[256,1024]{1,0:T(8,128)S(1)}, f32[256,1024]{1,0:T(8,128)S(1)}, f32[256,1024]{1,0:T(8,128)S(1)}, f32[8,256,1024]{2,1,0:T(8,128)}...) while((s32[]{:T(128)}, f32[256,1024]{1,0:T(8,128)S(1)}, ...), condition=%wide.region_3.4_spmd.clone, body=%wide.region_2.3_spmd.clone.sunk | while | flops 2621443 | bytes 13632135 | solution.py:112
  714.7 74.6 %all-gather.11.cloned.1.call-done = f32[4,256,1024]{2,1,0:T(8,128)} async-done(((f32[1,256,1024]{2,1,0:T(8,128)}), f32[4,256,1024]{2,1,0:T(8,128)}) %all-gather.11.cloned.1.call-update) | async-done | bytes 4194320 | tf_op jit(solution)/shard_map/all_gather | solution.py:21
  789.2 80.9 %all-gather.7.cloned.1.call-done = f32[4,256,1024]{2,1,0:T(8,128)} async-done(((f32[1,256,1024]{2,1,0:T(8,128)}), f32[4,256,1024]{2,1,0:T(8,128)}) %all-gather.7.cloned.1.call-update) | async-done | bytes 4194320 | tf_op jit(solution)/shard_map/all_gather | solution.py:21
  870.1 80.9 %all-gather.9.cloned.1.call-done = f32[4,256,1024]{2,1,0:T(8,128)} async-done(((f32[1,256,1024]{2,1,0:T(8,128)}), f32[4,256,1024]{2,1,0:T(8,128)}) %all-gather.9.cloned.1.call-update) | async-done | bytes 4194320 | tf_op jit(solution)/shard_map/all_gather | solution.py:21
  978.4 39.3 %while.113 = (s32[]{:T(128)}, f32[256,1024]{1,0:T(8,128)S(1)}, f32[256,1024]{1,0:T(8,128)S(1)}, f32[256,1024]{1,0:T(8,128)S(1)}, f32[8,256,1024]{2,1,0:T(8,128)}...) while((s32[]{:T(128)}, f32[256,1024]{1,0:T(8,128)S(1)}, ...), condition=%wide.region_7.8_spmd.clone, body=%wide.region_6.7_spmd.clone.sunk | while | flops 2097156 | bytes 12583063 | solution.py:130
  1024.8 82.7 %all-gather.13.cloned.1.call-done = f32[4,256,1024]{2,1,0:T(8,128)} async-done(((f32[1,256,1024]{2,1,0:T(8,128)}), f32[4,256,1024]{2,1,0:T(8,128)}) %all-gather.13.cloned.1.call-update) | async-done | bytes 4194320 | tf_op jit(solution)/shard_map/all_gather | solution.py:21
  1107.5 80.7 %all-gather.15.cloned.1.call-done = f32[4,256,1024]{2,1,0:T(8,128)} async-done(((f32[1,256,1024]{2,1,0:T(8,128)}), f32[4,256,1024]{2,1,0:T(8,128)}) %all-gather.15.cloned.1.call-update) | async-done | bytes 4194320 | tf_op jit(solution)/shard_map/all_gather | solution.py:21
  1188.2 80.7 %all-gather.17.cloned.1.call-done = f32[4,256,1024]{2,1,0:T(8,128)} async-done(((f32[1,256,1024]{2,1,0:T(8,128)}), f32[4,256,1024]{2,1,0:T(8,128)}) %all-gather.17.cloned.1.call-update) | async-done | bytes 4194320 | tf_op jit(solution)/shard_map/all_gather | solution.py:21
  1308.1 49.5 %fusion.87 = f32[8,1024,512]{1,2,0:T(8,128)} fusion(f32[8,512,1024]{2,1,0:T(8,128)} %pad_maximum_fusion.13), kind=kOutput, calls=%fused_computation.143 | convolution fusion | flops 25784483840 | bytes 33554432 | tf_op jit(solution)/shard_map/ky,zck->zyc/dot_general | solution.py:93
  1357.6 49.8 %fusion.88 = f32[8,1024,512]{1,2,0:T(8,128)} fusion(f32[8,512,1024]{2,1,0:T(8,128)} %pad_maximum_fusion.14), kind=kOutput, calls=%fused_computation.144 | convolution fusion | flops 25784483840 | bytes 33554432 | tf_op jit(solution)/shard_map/ky,zck->zyc/dot_general | solution.py:94
  1461.6 183.9 %all-to-all-done.1 = f32[8,1024,1,512]{3,0,2,1:T(8,128)} async-done(((f32[8,1024,1,512]{3,0,2,1:T(8,128)}), f32[8,1024,1,512]{3,0,2,1:T(8,128)}, u32[]{:S(2)}, u32[]{:S(2)}) %all-to-all-start.1) | async-done | bytes 16777248 | tf_op jit(solution)/shard_map/all_to_all | solution.py:186
  1681.5 229.9 %while.114 = (s32[]{:T(128)}, f32[8,128,2048]{2,1,0:T(8,128)}, f32[8,128,4096]{2,1,0:T(8,128)}, s32[]{:T(128)}, s32[]{:T(128)}, /*index=5*/s32[]{:T(128)}, s32[]{:T(128)}) while((s32[]{:T(128)}, f32[8,128,2048]{2,1,0:T(8,128)}, f32[8,128,4096]{2,1,0:T(8,128)}, s32[]{:T(128)}, s32[]{:T(128)}, /*index=5*/s32[]{:T(128)}, ...), condition=%wide.region_11.12_spmd.clone, body=%wide.region_10.11_spmd.clone.sunk | while | flops 6480217600 | bytes 18892948 | solution.py:72
  (149 shorter events, 646.8 us)
Async XLA Ops:
  7.6 17.0 copy-start.5
  7.6 16.8 collective-permute-start
  347.4 189.7 %all-to-all-start = ((f32[8,128,8,512]{1,3,0,2:T(8,128)}), f32[8,128,8,512]{1,3,0,2:T(8,128)}, u32[]{:S(2)}, u32[]{:S(2)}) async-start(f32[8,128,8,512]{1,3,0,2:T(8,128)} %copy.12), calls=%async_computation | async-start | bytes 33554432 | tf_op jit(solution)/shard_map/all_to_all | solution.py:167
  353.2 436.0 %all-gather.11.cloned.1.call-start = ((), (), s32[]{:S(2)}) async-start(), calls=%async_computation.4 | async-start | bytes 5242880 | tf_op jit(solution)/shard_map/all_gather | solution.py:21
  572.9 32.5 %copy-start.3 = (f32[8,1024,512]{1,2,0:T(8,128)S(1)}, f32[8,1024,512]{1,2,0:T(8,128)}, u32[]{:S(2)}) copy-start(f32[8,1024,512]{1,2,0:T(8,128)} %reshape.22) | copy-start | bytes 50331652
  572.9 32.5 %copy-start.4 = (f32[1024,1024,1]{1,0,2:T(8,128)S(1)}, f32[1024,1024,1]{1,0,2:T(8,128)}, u32[]{:S(2)}) copy-start(f32[1024,1024,1]{1,0,2:T(8,128)} %fusion.151) | copy-start | bytes 12582916
  709.8 160.4 %all-gather.7.cloned.1.call-start = ((), (), s32[]{:S(2)}) async-start(), calls=%async_computation.2 | async-start | bytes 5242880 | tf_op jit(solution)/shard_map/all_gather | solution.py:21
  712.2 238.9 %all-gather.9.cloned.1.call-start = ((), (), s32[]{:S(2)}) async-start(), calls=%async_computation.3 | async-start | bytes 5242880 | tf_op jit(solution)/shard_map/all_gather | solution.py:21
  714.6 392.9 %all-gather.13.cloned.1.call-start = ((), (), s32[]{:S(2)}) async-start(), calls=%async_computation.5 | async-start | bytes 5242880 | tf_op jit(solution)/shard_map/all_gather | solution.py:21
  969.7 8.6 copy-start.1
  969.7 8.6 copy-start.2
  1020.1 168.2 %all-gather.15.cloned.1.call-start = ((), (), s32[]{:S(2)}) async-start(), calls=%async_computation.6 | async-start | bytes 5242880 | tf_op jit(solution)/shard_map/all_gather | solution.py:21
  1022.4 246.6 %all-gather.17.cloned.1.call-start = ((), (), s32[]{:S(2)}) async-start(), calls=%async_computation.7 | async-start | bytes 5242880 | tf_op jit(solution)/shard_map/all_gather | solution.py:21
  1290.9 11.1 copy-start
  1455.9 189.7 %all-to-all-start.1 = ((f32[8,1024,1,512]{3,0,2,1:T(8,128)}), f32[8,1024,1,512]{3,0,2,1:T(8,128)}, u32[]{:S(2)}, u32[]{:S(2)}) async-start(f32[8,1024,1,512]{3,0,2,1:T(8,128)} %copy.14), calls=%async_computation.1 | async-start | bytes 33554432 | tf_op jit(solution)/shard_map/all_to_all | solution.py:186
Sparse Core Ops, SparseCore 0:
  709.9 79.2 all-gather.10
  790.8 79.2 all-gather.6
  871.7 79.2 all-gather.8
  1020.2 87.2 all-gather.12
  1108.9 79.2 all-gather.14
  1189.7 79.2 all-gather.16
where the time goes:
time: 1940 us; the launch traced here: 1930 us
  waiting for transfers between devices  825 us (43%)
  matrix products  686 us (35%)
  other arithmetic  231 us (12%)
  local copies, waits for them, and re-layouts  156 us (8%)
    all_gather x6, waiting for transfers between devices, entering(): gathered = jax.tree.map(lambda a: lax.all_gather(a, axis), part)  481 us
    dot_general x8, matrix products, advance(): jnp.einsum('zyn,nc->zyc', source, twiddle, precision=TWIDDLE_PRECISION)  295 us
    dot_general x8, matrix products, advance(): jnp.einsum('zyc,nc->zyn', column_piece, twiddle, precision=TWIDDLE_PRECIS...  230 us
    all_to_all x1, waiting for transfers between devices, on_device(): lax.all_to_all(stacked, 'gy', split_axis=1, concat_axis=2, tiled=True)  184 us
    all_to_all x1, waiting for transfers between devices, on_device(): lax.all_to_all(spectrum, 'gy', split_axis=2, concat_axis=1, tiled=True)  151 us
    dynamic_update_slice x16, other arithmetic, sweep_down(): lax.scan(advance, start_state, (cosine_component, imag_part, diagonal_div...  80.1 us
    dot_general x1, matrix products, back_span(): jnp.einsum('ky,zck->zyc', sine, stacked, precision=TWIDDLE_PRECISION)  49.8 us
    dot_general x1, matrix products, back_span(): jnp.einsum('ky,zck->zyc', cosine, stacked, precision=TWIDDLE_PRECISION)  49.5 us
  transfers between devices with their start and end apart: 9, of which 9 were waited for; matrix products, arithmetic and copies ran while one was open for 2% of the time, Pallas kernels for 0%

commit v1 on v0

v1 whole, which is shorter than its diff:
```python
import functools
import math

import jax
import jax.numpy as jnp
from jax import lax
from jax.experimental import pallas as pl
from jax.sharding import PartitionSpec as P

PREC = lax.Precision.HIGH
F32 = jnp.float32


def passed_along(x, axis, by):
    size = lax.axis_size(axis)
    pairs = [(i, i + by) for i in range(size) if 0 <= i + by < size]
    return lax.ppermute(x, axis, pairs)


def unit_circle(phase, count):
    angle = (phase % count).astype(F32) * (2.0 * math.pi / count)
    return jnp.cos(angle), jnp.sin(angle)


def circle_table(count):
    low = 32
    high = count // low
    k = jnp.arange(count, dtype=jnp.int32)[None, :]
    ch, sh = unit_circle(jnp.arange(high, dtype=jnp.int32)[:, None] * low * k, count)
    cl, sl = unit_circle(jnp.arange(low, dtype=jnp.int32)[:, None] * k, count)
    ch, sh, cl, sl = lax.optimization_barrier((ch, sh, cl, sl))
    ch, sh, cl, sl = ch[:, None], sh[:, None], cl[None], sl[None]
    cosine = (ch * cl - sh * sl).reshape(count, count)
    sine = (sh * cl + ch * sl).reshape(count, count)
    return cosine, sine


def split_table(count, half):
    low = 32
    column = jnp.arange(2 * count, dtype=jnp.int32)[None, :]
    k = column // (2 * half) * half + column % half
    quarter = jnp.where(column % (2 * half) < half, 0, count // 4)
    ch, sh = unit_circle(jnp.arange(count // low, dtype=jnp.int32)[:, None] * low * k, count)
    cl, sl = unit_circle(jnp.arange(low, dtype=jnp.int32)[:, None] * k + quarter, count)
    ch, sh, cl, sl = lax.optimization_barrier((ch, sh, cl, sl))
    return (ch[:, None] * cl[None] - sh[:, None] * sl[None]).reshape(count, 2 * count)


def down_kernel(chunks, per, *refs):
    cos_refs, sin_refs = refs[:chunks], refs[chunks : 2 * chunks]
    pivot, lower, low, summary = refs[2 * chunks :]
    re = im = jnp.zeros(pivot.shape[1:], F32)
    gain = jnp.ones(pivot.shape[1:], F32)
    for z in range(chunks * per):
        c, s = cos_refs[z // per], sin_refs[z // per]
        q = z % per
        d, m = pivot[z], lower[z]
        re = d * (c[q, 0] + s[q, 1]) + m * re
        im = d * (c[q, 1] - s[q, 0]) + m * im
        gain = m * gain
        low[z, 0] = re
        low[z, 1] = im
    summary[0] = gain
    summary[1] = re
    summary[2] = im


def up_summary_kernel(levels, low, lower, upper, enter, summary):
    er, ei = enter[0, 0], enter[0, 1]
    re = im = jnp.zeros(lower.shape[1:], F32)
    gain = jnp.ones(lower.shape[1:], F32)
    carried = jnp.ones(lower.shape[1:], F32)
    for z in range(levels):
        carried = carried * lower[z]
        re = re + gain * (low[z, 0] + carried * er)
        im = im + gain * (low[z, 1] + carried * ei)
        gain = gain * upper[z]
    summary[0] = gain
    summary[1] = re
    summary[2] = im


def solve_kernel(levels, per, low, lower, upper, enter, above, *outs):
    er, ei = enter[0, 0], enter[0, 1]
    gains = []
    carried = jnp.ones(lower.shape[1:], F32)
    for z in range(levels):
        carried = carried * lower[z]
        gains.append(carried)
    re, im = above[0, 0], above[0, 1]
    for z in range(levels - 1, -1, -1):
        re = low[z, 0] + gains[z] * er + upper[z] * re
        im = low[z, 1] + gains[z] * ei + upper[z] * im
        outs[z // per][z % per, 0] = re
        outs[z // per][z % per, 1] = im


def entering(summary, reverse):
    count = lax.axis_size("gz")
    _, width, span = summary.shape
    parts = summary.reshape(3, count, width // count, span)
    got = lax.all_to_all(parts, "gz", split_axis=1, concat_axis=1, tiled=True)
    order = list(range(count))
    if reverse:
        order.reverse()
    states = [None] * count
    state = jnp.zeros((2, width // count, span), F32)
    for at in order:
        states[at] = state
        state = got[1:, at] + got[0, at][None] * state
    return lax.all_to_all(jnp.stack(states), "gz", split_axis=0, concat_axis=0, tiled=True)


def on_device(
    pressure_cotangent,
    velocity_cotangent,
    inverse_spacing,
    inverse_pivot,
    lower_factor,
    upper_factor,
):
    levels, rows, nx = pressure_cotangent.shape
    level_above = passed_along(velocity_cotangent[:1], "gz", -1)
    gy = lax.axis_size("gy")
    gz = lax.axis_size("gz")
    ny = rows * gy
    half = nx // gy
    per = 2 if levels % 2 == 0 else 1
    chunks = levels // per
    velocity = velocity_cotangent.astype(F32)
    shifted = jnp.concatenate([velocity[1:], level_above.astype(F32)], 0)
    source = pressure_cotangent.astype(F32) + inverse_spacing[:, None, None] * (shifted - velocity)

    table = lax.optimization_barrier(split_table(nx, half))
    cy, sy = lax.optimization_barrier(circle_table(ny))

    cos_parts, sin_parts = [], []
    for i in range(chunks):
        piece = source[i * per : (i + 1) * per]
        spec = jnp.einsum("zyn,nc->zyc", piece, table, precision=PREC)
        spec = jnp.transpose(spec.reshape(per, rows, gy, 2 * half), (2, 0, 1, 3))
        got = lax.all_to_all(spec, "gy", split_axis=0, concat_axis=0, tiled=True)
        got = jnp.transpose(got, (1, 0, 2, 3)).reshape(per, ny, 2 * half)
        c = jnp.einsum("zyc,yk->zck", got, cy, precision=PREC)
        s = jnp.einsum("zyc,yk->zck", got, sy, precision=PREC)
        cos_parts.append(c.reshape(per, 2, half, ny))
        sin_parts.append(s.reshape(per, 2, half, ny))

    quarter = half // gz
    kb = min(16, quarter)
    in_quarter = quarter // kb
    grid = (half // kb,)
    chunk_spec = pl.BlockSpec((per, 2, kb, ny), lambda i: (0, 0, i, 0))
    factor_spec = pl.BlockSpec((levels, kb, ny), lambda i: (0, i, 0))
    low_spec = pl.BlockSpec((levels, 2, kb, ny), lambda i: (0, 0, i, 0))
    summary_spec = pl.BlockSpec((3, kb, ny), lambda i: (0, i, 0))
    state_spec = pl.BlockSpec((1, 2, kb, ny), lambda i: (i // in_quarter, 0, i % in_quarter, 0))
    summary_shape = jax.ShapeDtypeStruct((3, half, ny), F32)

    low, summary = pl.pallas_call(
        functools.partial(down_kernel, chunks, per),
        grid=grid,
        in_specs=[chunk_spec] * (2 * chunks) + [factor_spec] * 2,
        out_specs=[low_spec, summary_spec],
        out_shape=[jax.ShapeDtypeStruct((levels, 2, half, ny), F32), summary_shape],
    )(*cos_parts, *sin_parts, inverse_pivot, lower_factor)
    enter = entering(summary, False)
    summary = pl.pallas_call(
        functools.partial(up_summary_kernel, levels),
        grid=grid,
        in_specs=[low_spec, factor_spec, factor_spec, state_spec],
        out_specs=summary_spec,
        out_shape=summary_shape,
    )(low, lower_factor, upper_factor, enter)
    above = entering(summary, True)
    solved = pl.pallas_call(
        functools.partial(solve_kernel, levels, per),
        grid=grid,
        in_specs=[low_spec, factor_spec, factor_spec, state_spec, state_spec],
        out_specs=[chunk_spec] * chunks,
        out_shape=[jax.ShapeDtypeStruct((per, 2, half, ny), F32)] * chunks,
    )(low, lower_factor, upper_factor, enter, above)

    normalizer = 1.0 / (nx * ny)
    fields = []
    for i in range(chunks):
        flat = solved[i].reshape(per, 2 * half, ny)
        c = jnp.einsum("ky,zck->zyc", cy, flat, precision=PREC)
        s = jnp.einsum("ky,zck->zyc", sy, flat, precision=PREC)
        back = jnp.concatenate([c[..., :half] - s[..., half:], c[..., half:] + s[..., :half]], 2)
        back = jnp.transpose(back.reshape(per, gy, rows, 2 * half), (1, 0, 2, 3))
        got = lax.all_to_all(back, "gy", split_axis=0, concat_axis=0, tiled=True)
        got = jnp.transpose(got, (1, 2, 0, 3)).reshape(per, rows, 2 * nx)
        field = jnp.einsum("zyc,nc->zyn", got, table, precision=PREC) * normalizer
        fields.append(field.astype(jnp.bfloat16))
    return jnp.concatenate(fields, 0)


def solution(mesh):
    spec = P("gz", "gy", None)
    return jax.shard_map(
        on_device,
        mesh=mesh,
        in_specs=(spec, spec, P("gz"), spec, spec, spec),
        out_specs=spec,
        check_vma=False,
    )
```

time: 1940 us -> 939 us (0.48)
  waiting for transfers between devices: 825 us -> 113 us
  matrix products: 686 us -> 303 us
  blocking collectives: 0 us -> 252 us
  other arithmetic: 231 us -> 48 us
  Pallas kernels: 0 us -> 65 us
  local copies, waits for them, and re-layouts: 156 us -> 110 us
  starting transfers between devices: 13.2 us -> 39.7 us
    all_gather x6 -> x0, waiting for transfers between devices: 481 us -> none  [entering(): gathered = jax.tree.map(lambda a: lax.all_gather(a, axis), part)]
    dot_general x20 -> x24, matrix products: 686 us -> 303 us  [the longest x4 82.8 us: on_device(): spec = jnp.einsum('zyn,nc->zyc', piece, table, precision=PREC)]
    all_to_all x0 -> x4, blocking collectives: none -> 252 us  [the longest x2 151 us: entering(): got = lax.all_to_all(parts, 'gz', split_axis=1, concat_axis=1, tiled=True)]
    all_to_all x2 -> x8, waiting for transfers between devices: 335 us -> 113 us  [the longest x4 57.6 us: on_device(): got = lax.all_to_all(back, 'gy', split_axis=0, concat_axis=0, tiled=True)]
    dynamic_update_slice x16 -> x0, other arithmetic: 80.1 us -> none  [sweep_down(): lax.scan(advance, start_state, (cosine_component, imag_part, diagonal_div...]
    pallas_call x0 -> x3, Pallas kernels: none -> 65 us  [the longest x1 25.7 us: on_device(): pl.pallas_call(functools.partial(down_kernel, chunks, per), grid=grid, in...]
    dot_general x4 -> x0, other arithmetic: 49.3 us -> none  [the longest x1 16.3 us: along_span(): jnp.einsum('ky,zyc->zck', sine, stacked, precision=TWIDDLE_PRECISION)]
    add x6 -> x5, other arithmetic: 44.4 us -> 9.49 us  [the longest x1 4.47 us: circle_table(): sine = (sh * cl + ch * sl).reshape(count, count)]
  transfers between devices with their start and end apart: 9 -> 9, of which waited for: 9 -> 6; matrix products, arithmetic and copies ran while one was open for 2% -> 36% of each run, Pallas kernels for 0% -> 0%
where the time goes in v1:
time: 939 us; the launch traced here: 931 us
  matrix products  303 us (32%)
  blocking collectives  252 us (27%)
  waiting for transfers between devices  113 us (12%)
  local copies, waits for them, and re-layouts  110 us (12%)
  Pallas kernels  65 us (7%)
  other arithmetic  48 us (5%)
  starting transfers between devices  39.7 us (4%)
    all_to_all x2, blocking collectives, entering(): got = lax.all_to_all(parts, 'gz', split_axis=1, concat_axis=1, tiled=True)  151 us
    all_to_all x2, blocking collectives, entering(): lax.all_to_all(jnp.stack(states), 'gz', split_axis=0, concat_axis=0, tile...  102 us
    dot_general x4, matrix products, on_device(): spec = jnp.einsum('zyn,nc->zyc', piece, table, precision=PREC)  82.8 us
    dot_general x4, matrix products, on_device(): field = jnp.einsum('zyc,nc->zyn', got, table, precision=PREC) * normalizer  74.5 us
    all_to_all x4, waiting for transfers between devices, on_device(): got = lax.all_to_all(back, 'gy', split_axis=0, concat_axis=0, tiled=True)  57.6 us
    all_to_all x4, waiting for transfers between devices, on_device(): got = lax.all_to_all(spec, 'gy', split_axis=0, concat_axis=0, tiled=True)  55.1 us
    dot_general x4, matrix products, on_device(): c = jnp.einsum('ky,zck->zyc', cy, flat, precision=PREC)  42.4 us
    dot_general x4, matrix products, on_device(): s = jnp.einsum('zyc,yk->zck', got, sy, precision=PREC)  42.2 us
  transfers between devices with their start and end apart: 9, of which 6 were waited for; matrix products, arithmetic and copies ran while one was open for 36% of the time, Pallas kernels for 0%

profile of v1, /device:TPU:0, one launch (start us, length us, event | category | flops | bytes accessed | tf_op | source)
XLA Modules:
  0.0 931.1 jit_solution(7026945756558673726)
XLA Ops:
  8.6 12.0 %multiply_subtract_fusion = f32[64,32,4096]{2,1,0:T(8,128)} fusion(f32[32,4096]{1,0:T(8,128)S(1)} %get-tuple-element.24, f32[64,4096]{1,0:T(8,128)S(1)} %get-tuple-element.23, f32[32,4096]{1,0:T(8,128)S(1)} %get-tuple-element.22, f32[64,4096]{1,0:T(8,128)S(1)} %get-tuple-element.21), kind=kLoop, calls=%fused_computation.16 | loop fusion | flops 25165824 | bytes 36700160 | tf_op jit(solution)/shard_map/sub | solution.py:46
  27.2 20.7 %fusion.8 = f32[2,128,4096]{2,1,0:T(8,128)} fusion(f32[8,128,2048]{2,1,0:T(8,128)} %fusion.17, f32[2048,4096]{1,0:T(8,128)} %bitcast.270), kind=kOutput, calls=%fused_computation.8 | convolution fusion | flops 12884901888 | bytes 46137344 | tf_op jit(solution)/shard_map/zyn,nc->zyc/dot_general | solution.py:140
  57.9 20.7 %fusion.10 = f32[2,128,4096]{2,1,0:T(8,128)} fusion(f32[8,128,2048]{2,1,0:T(8,128)} %fusion.17, f32[2048,4096]{1,0:T(8,128)} %bitcast.271), kind=kOutput, calls=%fused_computation.10 | convolution fusion | flops 12884901888 | bytes 46137344 | tf_op jit(solution)/shard_map/zyn,nc->zyc/dot_general | solution.py:140
  83.4 23.7 %all-to-all-done.3 = f32[8,2,128,512]{3,2,1,0:T(8,128)} async-done(((f32[8,2,128,512]{3,2,1,0:T(8,128)}), f32[8,2,128,512]{3,2,1,0:T(8,128)}, u32[]{:S(2)}, u32[]{:S(2)}) %all-to-all-start.3) | async-done | bytes 4194336 | tf_op jit(solution)/shard_map/all_to_all | solution.py:142
  111.8 20.7 %fusion.12 = f32[2,128,4096]{2,1,0:T(8,128)} fusion(f32[8,128,2048]{2,1,0:T(8,128)} %fusion.17, f32[2048,4096]{1,0:T(8,128)} %bitcast.272), kind=kOutput, calls=%fused_computation.12 | convolution fusion | flops 12884901888 | bytes 46137344 | tf_op jit(solution)/shard_map/zyn,nc->zyc/dot_general | solution.py:140
  137.3 23.6 %all-to-all-done.2 = f32[8,2,128,512]{3,2,1,0:T(8,128)} async-done(((f32[8,2,128,512]{3,2,1,0:T(8,128)}), f32[8,2,128,512]{3,2,1,0:T(8,128)}, u32[]{:S(2)}, u32[]{:S(2)}) %all-to-all-start.2) | async-done | bytes 4194336 | tf_op jit(solution)/shard_map/all_to_all | solution.py:142
  171.1 20.7 %fusion.14 = f32[2,128,4096]{2,1,0:T(8,128)} fusion(f32[8,128,2048]{2,1,0:T(8,128)} %fusion.17, f32[2048,4096]{1,0:T(8,128)} %bitcast.273), kind=kOutput, calls=%fused_computation.14 | convolution fusion | flops 12884901888 | bytes 46137344 | tf_op jit(solution)/shard_map/zyn,nc->zyc/dot_general | solution.py:140
  219.5 11.2 %fusion.34.refs_7_ = f32[2,2,256,1024]{3,2,1,0:T(8,128)} fusion(f32[2,2,256,1024]{3,2,1,0:T(8,128)} %bitcast.307, f32[1024,1024]{1,0:T(8,128)} %bitcast.291), kind=kOutput, calls=%fused_computation.49 | convolution fusion | flops 6442450944 | bytes 12582912 | tf_op jit(solution)/shard_map/zyc,yk->zck/dot_general | solution.py:145
  251.0 11.2 %fusion.36.refs_6_ = f32[2,2,256,1024]{3,2,1,0:T(8,128)} fusion(f32[2,2,256,1024]{3,2,1,0:T(8,128)} %bitcast.309, f32[1024,1024]{1,0:T(8,128)} %bitcast.292), kind=kOutput, calls=%fused_computation.51 | convolution fusion | flops 6442450944 | bytes 12582912 | tf_op jit(solution)/shard_map/zyc,yk->zck/dot_general | solution.py:145
  306.1 11.5 %fusion.40.refs_4_ = f32[2,2,256,1024]{3,2,1,0:T(8,128)} fusion(f32[2,2,256,1024]{3,2,1,0:T(8,128)} %bitcast.313, f32[1024,1024]{1,0:T(8,128)} %bitcast.293), kind=kOutput, calls=%fused_computation.55 | convolution fusion | flops 6442450944 | bytes 12582912 | tf_op jit(solution)/shard_map/zyc,yk->zck/dot_general | solution.py:145
  325.8 25.7 %shard_map.64 = (f32[8,2,256,1024]{3,2,1,0:T(8,128)}, f32[3,256,1024]{2,1,0:T(8,128)}) custom-call(f32[2,2,256,1024]{3,2,1,0:T(8,128)} %fusion.48.refs_0_, f32[2,2,256,1024]{3,2,1,0:T(8,128)} %fusion.46.refs_1_, f32[2,2,256,1024]{3,2,1,0:T(8,128)} %fusion.44.refs_2_, f32[2,2,256,1024]{3,2,1,0:T(8,128)} %fusion.42.refs_3_, ...), custom_call_target="tpu_custom_call" | custom-call | tf_op jit(solution)/shard_map/pallas_call | solution.py:160
  353.7 77.8 %all_to_all.60 = f32[3,4,64,1024]{3,2,0,1:T(8,128)S(1)} all-to-all(f32[3,4,64,1024]{3,2,0,1:T(8,128)S(1)} %copy.37), channel_id=1, replica_groups=mesh['gy'=8,'gz'=4] {'gz'}, dimensions={1} | all-to-all | bytes 6291456 | tf_op jit(solution)/shard_map/all_to_all | solution.py:102
  432.1 51.2 %all_to_all.61.enter = f32[4,2,64,1024]{3,2,1,0:T(8,128)} all-to-all(f32[4,2,64,1024]{3,2,1,0:T(8,128)S(1)} %pad_maximum_fusion.1), channel_id=1, replica_groups=mesh['gy'=8,'gz'=4] {'gz'}, dimensions={0} | all-to-all | bytes 4194304 | tf_op jit(solution)/shard_map/all_to_all | solution.py:111
  483.4 17.1 %shard_map.65 = f32[3,256,1024]{2,1,0:T(8,128)} custom-call(f32[8,2,256,1024]{3,2,1,0:T(8,128)} %get-tuple-element.31.low, f32[8,256,1024]{2,1,0:T(8,128)} %lower.3, f32[8,256,1024]{2,1,0:T(8,128)} %upper.3, f32[4,2,64,1024]{3,2,1,0:T(8,128)} %all_to_all.61.enter), custom_call_target="tpu_custom_call" | custom-call | tf_op jit(solution)/shard_map/pallas_call | solution.py:168
  502.6 72.7 %all_to_all.62 = f32[3,4,64,1024]{3,2,0,1:T(8,128)S(1)} all-to-all(f32[3,4,64,1024]{3,2,0,1:T(8,128)S(1)} %copy.38), channel_id=1, replica_groups=mesh['gy'=8,'gz'=4] {'gz'}, dimensions={1} | all-to-all | bytes 6291456 | tf_op jit(solution)/shard_map/all_to_all | solution.py:102
  575.9 50.7 %all_to_all.63.above = f32[4,2,64,1024]{3,2,1,0:T(8,128)} all-to-all(f32[4,2,64,1024]{3,2,1,0:T(8,128)S(1)} %pad_maximum_fusion.2), channel_id=1, replica_groups=mesh['gy'=8,'gz'=4] {'gz'}, dimensions={0} | all-to-all | bytes 4194304 | tf_op jit(solution)/shard_map/all_to_all | solution.py:111
  626.6 22.1 %shard_map.66 = (f32[2,2,256,1024]{3,2,1,0:T(8,128)}, f32[2,2,256,1024]{3,2,1,0:T(8,128)}, f32[2,2,256,1024]{3,2,1,0:T(8,128)}, f32[2,2,256,1024]{3,2,1,0:T(8,128)}) custom-call(f32[8,2,256,1024]{3,2,1,0:T(8,128)} %get-tuple-element.31.low, f32[8,256,1024]{2,1,0:T(8,128)} %lower.3, f32[8,256,1024]{2,1,0:T(8,128)} %upper.3, ...), custom_call_target="tpu_custom_call" | custom-call | tf_op jit(solution)/shard_map/pallas_call | solution.py:176
  696.4 27.8 %all-to-all-done.8 = f32[8,2,128,512]{2,3,1,0:T(8,128)} async-done(((f32[8,2,128,512]{2,3,1,0:T(8,128)}), f32[8,2,128,512]{2,3,1,0:T(8,128)}, u32[]{:S(2)}, u32[]{:S(2)}) %all-to-all-start.8) | async-done | bytes 4194336 | tf_op jit(solution)/shard_map/all_to_all | solution.py:192
  729.0 10.6 %fusion.80 = f32[2,1024,512]{1,2,0:T(8,128)S(1)} fusion(f32[2,512,1024]{2,1,0:T(8,128)} %bitcast.318, f32[1024,1024]{1,0:T(8,128)} %bitcast.301), kind=kOutput, calls=%fused_computation.77 | convolution fusion | flops 6442450944 | bytes 12582912 | tf_op jit(solution)/shard_map/ky,zck->zyc/dot_general | solution.py:188
  750.3 27.8 %all-to-all-done.9 = f32[8,2,128,512]{2,3,1,0:T(8,128)} async-done(((f32[8,2,128,512]{2,3,1,0:T(8,128)}), f32[8,2,128,512]{2,3,1,0:T(8,128)}, u32[]{:S(2)}, u32[]{:S(2)}) %all-to-all-start.9) | async-done | bytes 4194336 | tf_op jit(solution)/shard_map/all_to_all | solution.py:192
  825.6 18.3 %fusion.71 = bf16[2,128,2048]{2,1,0:T(8,128)(2,1)S(1)} fusion(f32[2,128,4096]{2,1,0:T(8,128)} %reshape.317, f32[2048,4096]{1,0:T(8,128)} %bitcast.274), kind=kOutput, calls=%fused_computation.74 | convolution fusion | flops 12885950464 | bytes 38797312 | tf_op jit(solution)/shard_map/zyc,nc->zyn/dot_general | solution.py:194
  859.1 18.3 %fusion.68 = bf16[2,128,2048]{2,1,0:T(8,128)(2,1)S(1)} fusion(f32[2,128,4096]{2,1,0:T(8,128)} %reshape.320, f32[2048,4096]{1,0:T(8,128)} %bitcast.275), kind=kOutput, calls=%fused_computation.73 | convolution fusion | flops 12885950464 | bytes 38797312 | tf_op jit(solution)/shard_map/zyc,nc->zyn/dot_general | solution.py:194
  877.4 18.3 %fusion.65 = bf16[2,128,2048]{2,1,0:T(8,128)(2,1)S(1)} fusion(f32[2,128,4096]{2,1,0:T(8,128)} %reshape.323, f32[2048,4096]{1,0:T(8,128)} %bitcast.276), kind=kOutput, calls=%fused_computation.72 | convolution fusion | flops 12885950464 | bytes 38797312 | tf_op jit(solution)/shard_map/zyc,nc->zyn/dot_general | solution.py:194
  908.1 19.5 %fusion.62 = bf16[2,128,2048]{2,1,0:T(8,128)(2,1)} fusion(f32[2,128,4096]{2,1,0:T(8,128)} %reshape.326, f32[2048,4096]{1,0:T(8,128)} %bitcast.277), kind=kOutput, calls=%fused_computation.71 | convolution fusion | flops 12885950464 | bytes 38797312 | tf_op jit(solution)/shard_map/zyc,nc->zyn/dot_general | solution.py:194
  (112 shorter events, 296.3 us)
Async XLA Ops:
  1.1 20.5 %collective-permute-start = (bf16[1,128,2048]{2,1,0:T(8,128)(2,1)S(1)}, bf16[1,128,2048]{2,1,0:T(8,128)(2,1)S(1)}, u32[]{:S(2)}, u32[]{:S(2)}) collective-permute-start(bf16[1,128,2048]{2,1,0:T(8,128)(2,1)S(1)} %slice.103), channel_id=1, source_target_pairs={{1,0},{2,1},{3,2},{5,4},{6,5},{7,6},{9,8},{10,9},{11,10},{13,12},{... | collective-permute-start | bytes 1572872 | tf_op jit(solution)/shard_map/ppermute | solution.py:17
  8.6 12.0 %copy-start = (bf16[8,128,2048]{2,1,0:T(8,128)(2,1)S(1)}, bf16[8,128,2048]{2,1,0:T(8,128)(2,1)}, u32[]{:S(2)}) copy-start(bf16[8,128,2048]{2,1,0:T(8,128)(2,1)} %param.7) | copy-start | bytes 12582916
  52.7 54.4 %all-to-all-start.3 = ((f32[8,2,128,512]{3,2,1,0:T(8,128)}), f32[8,2,128,512]{3,2,1,0:T(8,128)}, u32[]{:S(2)}, u32[]{:S(2)}) async-start(f32[8,2,128,512]{3,2,1,0:T(8,128)} %bitcast.281), calls=%async_computation.3 | async-start | bytes 8388608 | tf_op jit(solution)/shard_map/all_to_all | solution.py:142
  107.1 53.9 %all-to-all-start.2 = ((f32[8,2,128,512]{3,2,1,0:T(8,128)}), f32[8,2,128,512]{3,2,1,0:T(8,128)}, u32[]{:S(2)}, u32[]{:S(2)}) async-start(f32[8,2,128,512]{3,2,1,0:T(8,128)} %bitcast.280), calls=%async_computation.2 | async-start | bytes 8388608 | tf_op jit(solution)/shard_map/all_to_all | solution.py:142
  161.0 53.7 %all-to-all-start.1 = ((f32[8,2,128,512]{3,2,1,0:T(8,128)}), f32[8,2,128,512]{3,2,1,0:T(8,128)}, u32[]{:S(2)}, u32[]{:S(2)}) async-start(f32[8,2,128,512]{3,2,1,0:T(8,128)} %bitcast.278), calls=%async_computation.1 | async-start | bytes 8388608 | tf_op jit(solution)/shard_map/all_to_all | solution.py:142
  214.6 81.2 %all-to-all-start = ((f32[8,2,128,512]{3,2,1,0:T(8,128)}), f32[8,2,128,512]{3,2,1,0:T(8,128)}, u32[]{:S(2)}, u32[]{:S(2)}) async-start(f32[8,2,128,512]{3,2,1,0:T(8,128)} %bitcast.279), calls=%async_computation | async-start | bytes 8388608 | tf_op jit(solution)/shard_map/all_to_all | solution.py:142
  251.0 11.2 %copy-start.6 = (f32[32,32,1024]{2,1,0:T(8,128)S(1)}, f32[32,32,1024]{2,1,0:T(8,128)}, u32[]{:S(2)}) copy-start(f32[32,32,1024]{2,1,0:T(8,128)} %get-tuple-element.58) | copy-start | bytes 12582916
  251.0 11.2 %copy-start.8 = (f32[2,512,1024]{2,1,0:T(8,128)S(1)}, f32[2,512,1024]{2,1,0:T(8,128)}, u32[]{:S(2)}) copy-start(f32[2,512,1024]{2,1,0:T(8,128)} %copy.36) | copy-start | bytes 12582916
  270.6 8.7 copy-start.1
  270.6 8.7 copy-start.10
  306.1 11.5 %copy-start.7 = (f32[32,32,1024]{2,1,0:T(8,128)S(1)}, f32[32,32,1024]{2,1,0:T(8,128)}, u32[]{:S(2)}) copy-start(f32[32,32,1024]{2,1,0:T(8,128)} %get-tuple-element.58) | copy-start | bytes 12582916
  306.1 11.5 %copy-start.11 = (f32[2,512,1024]{2,1,0:T(8,128)S(1)}, f32[2,512,1024]{2,1,0:T(8,128)}, u32[]{:S(2)}) copy-start(f32[2,512,1024]{2,1,0:T(8,128)} %copy.27) | copy-start | bytes 12582916
  648.8 10.6 %copy-start.2 = (f32[32,32,1024]{2,1,0:T(8,128)S(1)}, f32[32,32,1024]{2,1,0:T(8,128)}, u32[]{:S(2)}) copy-start(f32[32,32,1024]{2,1,0:T(8,128)} %get-tuple-element.57) | copy-start | bytes 12582916
  648.8 10.6 %copy-start.17 = (f32[2,2,256,1024]{3,2,1,0:T(8,128)S(1)}, f32[2,2,256,1024]{3,2,1,0:T(8,128)}, u32[]{:S(2)}) copy-start(f32[2,2,256,1024]{3,2,1,0:T(8,128)} %get-tuple-element.33) | copy-start | bytes 12582916
  670.2 54.1 %all-to-all-start.8 = ((f32[8,2,128,512]{2,3,1,0:T(8,128)}), f32[8,2,128,512]{2,3,1,0:T(8,128)}, u32[]{:S(2)}, u32[]{:S(2)}) async-start(f32[8,2,128,512]{2,3,1,0:T(8,128)} %bitcast_bitcast_fusion.3), calls=%async_computation.8 | async-start | bytes 8388608 | tf_op jit(solution)/shard_map/all_to_all | solution.py:192
  675.1 10.6 %copy-start.3 = (f32[32,32,1024]{2,1,0:T(8,128)S(1)}, f32[32,32,1024]{2,1,0:T(8,128)}, u32[]{:S(2)}) copy-start(f32[32,32,1024]{2,1,0:T(8,128)} %get-tuple-element.57) | copy-start | bytes 12582916
  675.1 10.6 %copy-start.16 = (f32[2,2,256,1024]{3,2,1,0:T(8,128)S(1)}, f32[2,2,256,1024]{3,2,1,0:T(8,128)}, u32[]{:S(2)}) copy-start(f32[2,2,256,1024]{3,2,1,0:T(8,128)} %get-tuple-element.34) | copy-start | bytes 12582916
  724.3 53.9 %all-to-all-start.9 = ((f32[8,2,128,512]{2,3,1,0:T(8,128)}), f32[8,2,128,512]{2,3,1,0:T(8,128)}, u32[]{:S(2)}, u32[]{:S(2)}) async-start(f32[8,2,128,512]{2,3,1,0:T(8,128)} %bitcast_bitcast_fusion.2), calls=%async_computation.9 | async-start | bytes 8388608 | tf_op jit(solution)/shard_map/all_to_all | solution.py:192
  729.0 10.6 %copy-start.4 = (f32[32,32,1024]{2,1,0:T(8,128)S(1)}, f32[32,32,1024]{2,1,0:T(8,128)}, u32[]{:S(2)}) copy-start(f32[32,32,1024]{2,1,0:T(8,128)} %get-tuple-element.57) | copy-start | bytes 12582916
  729.0 10.6 %copy-start.15 = (f32[2,2,256,1024]{3,2,1,0:T(8,128)S(1)}, f32[2,2,256,1024]{3,2,1,0:T(8,128)}, u32[]{:S(2)}) copy-start(f32[2,2,256,1024]{3,2,1,0:T(8,128)} %get-tuple-element.35) | copy-start | bytes 12582916
  778.1 65.8 %all-to-all-start.10 = ((f32[8,2,128,512]{2,3,1,0:T(8,128)}), f32[8,2,128,512]{2,3,1,0:T(8,128)}, u32[]{:S(2)}, u32[]{:S(2)}) async-start(f32[8,2,128,512]{2,3,1,0:T(8,128)} %bitcast_bitcast_fusion.1), calls=%async_computation.10 | async-start | bytes 8388608 | tf_op jit(solution)/shard_map/all_to_all | solution.py:192
  782.9 10.6 %copy-start.5 = (f32[32,32,1024]{2,1,0:T(8,128)S(1)}, f32[32,32,1024]{2,1,0:T(8,128)}, u32[]{:S(2)}) copy-start(f32[32,32,1024]{2,1,0:T(8,128)} %get-tuple-element.57) | copy-start | bytes 12582916
  782.9 10.6 %copy-start.14 = (f32[2,2,256,1024]{3,2,1,0:T(8,128)S(1)}, f32[2,2,256,1024]{3,2,1,0:T(8,128)}, u32[]{:S(2)}) copy-start(f32[2,2,256,1024]{3,2,1,0:T(8,128)} %get-tuple-element.36) | copy-start | bytes 12582916
  843.9 53.7 %all-to-all-start.11 = ((f32[8,2,128,512]{2,3,1,0:T(8,128)}), f32[8,2,128,512]{2,3,1,0:T(8,128)}, u32[]{:S(2)}, u32[]{:S(2)}) async-start(f32[8,2,128,512]{2,3,1,0:T(8,128)} %bitcast_bitcast_fusion), calls=%async_computation.11 | async-start | bytes 8388608 | tf_op jit(solution)/shard_map/all_to_all | solution.py:192
  (3 other events, 12.7 us)

commit v2 on v1

--- a/solution.py
+++ b/solution.py
@@ -139,6 +139,10 @@
         piece = source[i * per : (i + 1) * per]
         spec = jnp.einsum("zyn,nc->zyc", piece, table, precision=PREC)
         spec = jnp.transpose(spec.reshape(per, rows, gy, 2 * half), (2, 0, 1, 3))
+        if i >= 2:
+            spec, cos_parts[i - 2], sin_parts[i - 2] = lax.optimization_barrier(
+                (spec, cos_parts[i - 2], sin_parts[i - 2])
+            )
         got = lax.all_to_all(spec, "gy", split_axis=0, concat_axis=0, tiled=True)
         got = jnp.transpose(got, (1, 0, 2, 3)).reshape(per, ny, 2 * half)
         c = jnp.einsum("zyc,yk->zck", got, cy, precision=PREC)
@@ -189,6 +193,8 @@
         s = jnp.einsum("ky,zck->zyc", sy, flat, precision=PREC)
         back = jnp.concatenate([c[..., :half] - s[..., half:], c[..., half:] + s[..., :half]], 2)
         back = jnp.transpose(back.reshape(per, gy, rows, 2 * half), (1, 0, 2, 3))
+        if i >= 2:
+            back, fields[i - 2] = lax.optimization_barrier((back, fields[i - 2]))
         got = lax.all_to_all(back, "gy", split_axis=0, concat_axis=0, tiled=True)
         got = jnp.transpose(got, (1, 2, 0, 3)).reshape(per, rows, 2 * nx)
         field = jnp.einsum("zyc,nc->zyn", got, table, precision=PREC) * normalizer

time: 939 us -> 916 us (0.976)
  waiting for transfers between devices: 113 us -> 90.6 us
    all_to_all x4, waiting for transfers between devices: 55.1 us -> 42.5 us  [on_device(): got = lax.all_to_all(spec, 'gy', split_axis=0, concat_axis=0, tiled=True)]
    all_to_all x4, waiting for transfers between devices: 57.6 us -> 48.1 us  [on_device(): got = lax.all_to_all(back, 'gy', split_axis=0, concat_axis=0, tiled=True)]
  transfers between devices with their start and end apart: 9 -> 9, of which waited for: 6 -> 4; matrix products, arithmetic and copies ran while one was open for 36% -> 38% of each run, Pallas kernels for 0% -> 0%
where the time goes in v2:
time: 916 us; the launch traced here: 908 us
  matrix products  306 us (33%)
  blocking collectives  247 us (27%)
  local copies, waits for them, and re-layouts  110 us (12%)
  waiting for transfers between devices  90.6 us (10%)
  Pallas kernels  64.9 us (7%)
  other arithmetic  47.7 us (5%)
  starting transfers between devices  42.5 us (5%)
    all_to_all x2, blocking collectives, entering(): got = lax.all_to_all(parts, 'gz', split_axis=1, concat_axis=1, tiled=True)  146 us
    all_to_all x2, blocking collectives, entering(): lax.all_to_all(jnp.stack(states), 'gz', split_axis=0, concat_axis=0, tile...  100 us
    dot_general x4, matrix products, on_device(): spec = jnp.einsum('zyn,nc->zyc', piece, table, precision=PREC)  82.8 us
    dot_general x4, matrix products, on_device(): field = jnp.einsum('zyc,nc->zyn', got, table, precision=PREC) * normalizer  74.6 us
    all_to_all x4, waiting for transfers between devices, on_device(): got = lax.all_to_all(back, 'gy', split_axis=0, concat_axis=0, tiled=True)  48.1 us
    dot_general x4, matrix products, on_device(): s = jnp.einsum('zyc,yk->zck', got, sy, precision=PREC)  45.1 us
    all_to_all x4, waiting for transfers between devices, on_device(): got = lax.all_to_all(spec, 'gy', split_axis=0, concat_axis=0, tiled=True)  42.5 us
    dot_general x4, matrix products, on_device(): c = jnp.einsum('ky,zck->zyc', cy, flat, precision=PREC)  42.4 us
  transfers between devices with their start and end apart: 9, of which 4 were waited for; matrix products, arithmetic and copies ran while one was open for 38% of the time, Pallas kernels for 0%

profile of v2, /device:TPU:0, one launch (start us, length us, event | category | flops | bytes accessed | tf_op | source)
XLA Modules:
  0.0 908.2 jit_solution(5228510412449788988)
XLA Ops:
  8.6 11.6 %multiply_subtract_fusion = f32[64,32,4096]{2,1,0:T(8,128)} fusion(f32[32,4096]{1,0:T(8,128)S(1)} %get-tuple-element.34, f32[64,4096]{1,0:T(8,128)S(1)} %get-tuple-element.33, f32[32,4096]{1,0:T(8,128)S(1)} %get-tuple-element.32, f32[64,4096]{1,0:T(8,128)S(1)} %get-tuple-element.31), kind=kLoop, calls=%fused_computation.16 | loop fusion | flops 25165824 | bytes 36700160 | tf_op jit(solution)/shard_map/sub | solution.py:46
  26.8 20.7 %fusion.8 = f32[2,128,4096]{2,1,0:T(8,128)} fusion(f32[8,128,2048]{2,1,0:T(8,128)} %fusion.17, f32[2048,4096]{1,0:T(8,128)} %bitcast.270), kind=kOutput, calls=%fused_computation.8 | convolution fusion | flops 12884901888 | bytes 46137344 | tf_op jit(solution)/shard_map/zyn,nc->zyc/dot_general | solution.py:140
  58.1 20.7 %fusion.12 = f32[2,128,4096]{2,1,0:T(8,128)} fusion(f32[8,128,2048]{2,1,0:T(8,128)} %fusion.17, f32[2048,4096]{1,0:T(8,128)} %bitcast.271), kind=kOutput, calls=%fused_computation.12 | convolution fusion | flops 12884901888 | bytes 46137344 | tf_op jit(solution)/shard_map/zyn,nc->zyc/dot_general | solution.py:140
  83.6 23.1 %all-to-all-done.1 = f32[8,2,128,512]{3,2,1,0:T(8,128)} async-done(((f32[8,2,128,512]{3,2,1,0:T(8,128)}), f32[8,2,128,512]{3,2,1,0:T(8,128)}, u32[]{:S(2)}, u32[]{:S(2)}) %all-to-all-start.1) | async-done | bytes 4194336 | tf_op jit(solution)/shard_map/all_to_all | solution.py:146
  116.6 20.7 %fusion.10 = f32[2,128,4096]{2,1,0:T(8,128)} fusion(f32[8,128,2048]{2,1,0:T(8,128)} %fusion.17, f32[2048,4096]{1,0:T(8,128)} %bitcast.272), kind=kOutput, calls=%fused_computation.10 | convolution fusion | flops 12884901888 | bytes 46137344 | tf_op jit(solution)/shard_map/zyn,nc->zyc/dot_general | solution.py:140
  152.3 11.3 %fusion.38.refs_5_ = f32[2,2,256,1024]{3,2,1,0:T(8,128)} fusion(f32[2,2,256,1024]{3,2,1,0:T(8,128)} %bitcast.307, f32[1024,1024]{1,0:T(8,128)} %bitcast.291), kind=kOutput, calls=%fused_computation.53 | convolution fusion | flops 6442450944 | bytes 12582912 | tf_op jit(solution)/shard_map/zyc,yk->zck/dot_general | solution.py:149
  176.6 20.7 %fusion.14 = f32[2,128,4096]{2,1,0:T(8,128)} fusion(f32[8,128,2048]{2,1,0:T(8,128)} %fusion.17, f32[2048,4096]{1,0:T(8,128)} %bitcast.273), kind=kOutput, calls=%fused_computation.14 | convolution fusion | flops 12884901888 | bytes 46137344 | tf_op jit(solution)/shard_map/zyn,nc->zyc/dot_general | solution.py:140
  212.5 11.3 %fusion.40.refs_4_ = f32[2,2,256,1024]{3,2,1,0:T(8,128)} fusion(f32[2,2,256,1024]{3,2,1,0:T(8,128)} %bitcast.309, f32[1024,1024]{1,0:T(8,128)} %bitcast.292), kind=kOutput, calls=%fused_computation.55 | convolution fusion | flops 6442450944 | bytes 12582912 | tf_op jit(solution)/shard_map/zyc,yk->zck/dot_general | solution.py:149
  247.3 11.3 %fusion.34.refs_7_ = f32[2,2,256,1024]{3,2,1,0:T(8,128)} fusion(f32[2,2,256,1024]{3,2,1,0:T(8,128)} %bitcast.311, f32[1024,1024]{1,0:T(8,128)} %bitcast.293), kind=kOutput, calls=%fused_computation.49 | convolution fusion | flops 6442450944 | bytes 12582912 | tf_op jit(solution)/shard_map/zyc,yk->zck/dot_general | solution.py:149
  266.8 19.3 %all-to-all-done.2 = f32[8,2,128,512]{3,2,1,0:T(8,128)} async-done(((f32[8,2,128,512]{3,2,1,0:T(8,128)}), f32[8,2,128,512]{3,2,1,0:T(8,128)}, u32[]{:S(2)}, u32[]{:S(2)}) %all-to-all-start.2) | async-done | bytes 4194336 | tf_op jit(solution)/shard_map/all_to_all | solution.py:146
  296.5 11.2 %fusion.36.refs_6_ = f32[2,2,256,1024]{3,2,1,0:T(8,128)} fusion(f32[2,2,256,1024]{3,2,1,0:T(8,128)} %bitcast.313, f32[1024,1024]{1,0:T(8,128)} %bitcast.294), kind=kOutput, calls=%fused_computation.51 | convolution fusion | flops 6442450944 | bytes 12582912 | tf_op jit(solution)/shard_map/zyc,yk->zck/dot_general | solution.py:149
  316.1 25.7 %shard_map.64 = (f32[8,2,256,1024]{3,2,1,0:T(8,128)}, f32[3,256,1024]{2,1,0:T(8,128)}) custom-call(f32[2,2,256,1024]{3,2,1,0:T(8,128)} %fusion.48.refs_0_, f32[2,2,256,1024]{3,2,1,0:T(8,128)} %fusion.46.refs_1_, f32[2,2,256,1024]{3,2,1,0:T(8,128)} %fusion.44.refs_2_, f32[2,2,256,1024]{3,2,1,0:T(8,128)} %fusion.42.refs_3_, ...), custom_call_target="tpu_custom_call" | custom-call | tf_op jit(solution)/shard_map/pallas_call | solution.py:164
  343.9 74.2 %all_to_all.60 = f32[3,4,64,1024]{3,2,0,1:T(8,128)S(1)} all-to-all(f32[3,4,64,1024]{3,2,0,1:T(8,128)S(1)} %copy.37), channel_id=1, replica_groups=mesh['gy'=8,'gz'=4] {'gz'}, dimensions={1} | all-to-all | bytes 6291456 | tf_op jit(solution)/shard_map/all_to_all | solution.py:102
  418.8 49.8 %all_to_all.61.enter = f32[4,2,64,1024]{3,2,1,0:T(8,128)} all-to-all(f32[4,2,64,1024]{3,2,1,0:T(8,128)S(1)} %pad_maximum_fusion.1), channel_id=1, replica_groups=mesh['gy'=8,'gz'=4] {'gz'}, dimensions={0} | all-to-all | bytes 4194304 | tf_op jit(solution)/shard_map/all_to_all | solution.py:111
  468.6 17.1 %shard_map.65 = f32[3,256,1024]{2,1,0:T(8,128)} custom-call(f32[8,2,256,1024]{3,2,1,0:T(8,128)} %get-tuple-element.47.low, f32[8,256,1024]{2,1,0:T(8,128)} %lower.3, f32[8,256,1024]{2,1,0:T(8,128)} %upper.3, f32[4,2,64,1024]{3,2,1,0:T(8,128)} %all_to_all.61.enter), custom_call_target="tpu_custom_call" | custom-call | tf_op jit(solution)/shard_map/pallas_call | solution.py:172
  487.8 72.1 %all_to_all.62 = f32[3,4,64,1024]{3,2,0,1:T(8,128)S(1)} all-to-all(f32[3,4,64,1024]{3,2,0,1:T(8,128)S(1)} %copy.38), channel_id=1, replica_groups=mesh['gy'=8,'gz'=4] {'gz'}, dimensions={1} | all-to-all | bytes 6291456 | tf_op jit(solution)/shard_map/all_to_all | solution.py:102
  560.5 50.6 %all_to_all.63.above = f32[4,2,64,1024]{3,2,1,0:T(8,128)} all-to-all(f32[4,2,64,1024]{3,2,1,0:T(8,128)S(1)} %pad_maximum_fusion.2), channel_id=1, replica_groups=mesh['gy'=8,'gz'=4] {'gz'}, dimensions={0} | all-to-all | bytes 4194304 | tf_op jit(solution)/shard_map/all_to_all | solution.py:111
  611.1 22.1 %shard_map.66 = (f32[2,2,256,1024]{3,2,1,0:T(8,128)}, f32[2,2,256,1024]{3,2,1,0:T(8,128)}, f32[2,2,256,1024]{3,2,1,0:T(8,128)}, f32[2,2,256,1024]{3,2,1,0:T(8,128)}) custom-call(f32[8,2,256,1024]{3,2,1,0:T(8,128)} %get-tuple-element.47.low, f32[8,256,1024]{2,1,0:T(8,128)} %lower.3, f32[8,256,1024]{2,1,0:T(8,128)} %upper.3, ...), custom_call_target="tpu_custom_call" | custom-call | tf_op jit(solution)/shard_map/pallas_call | solution.py:180
  683.0 27.8 %all-to-all-done.8 = f32[8,2,128,512]{2,3,1,0:T(8,128)} async-done(((f32[8,2,128,512]{2,3,1,0:T(8,128)}), f32[8,2,128,512]{2,3,1,0:T(8,128)}, u32[]{:S(2)}, u32[]{:S(2)}) %all-to-all-start.8) | async-done | bytes 4194336 | tf_op jit(solution)/shard_map/all_to_all | solution.py:198
  747.8 18.5 %fusion.71 = bf16[2,128,2048]{2,1,0:T(8,128)(2,1)S(1)} fusion(f32[2,128,4096]{2,1,0:T(8,128)} %reshape.319, f32[2048,4096]{1,0:T(8,128)} %bitcast.274), kind=kOutput, calls=%fused_computation.74 | convolution fusion | flops 12885950464 | bytes 38797312 | tf_op jit(solution)/shard_map/zyc,nc->zyn/dot_general | solution.py:200
  802.7 18.5 %fusion.68 = bf16[2,128,2048]{2,1,0:T(8,128)(2,1)S(1)} fusion(f32[2,128,4096]{2,1,0:T(8,128)} %reshape.324, f32[2048,4096]{1,0:T(8,128)} %bitcast.275), kind=kOutput, calls=%fused_computation.73 | convolution fusion | flops 12885950464 | bytes 38797312 | tf_op jit(solution)/shard_map/zyc,nc->zyn/dot_general | solution.py:200
  836.3 18.3 %fusion.65 = bf16[2,128,2048]{2,1,0:T(8,128)(2,1)S(1)} fusion(f32[2,128,4096]{2,1,0:T(8,128)} %reshape.325, f32[2048,4096]{1,0:T(8,128)} %bitcast.276), kind=kOutput, calls=%fused_computation.72 | convolution fusion | flops 12885950464 | bytes 38797312 | tf_op jit(solution)/shard_map/zyc,nc->zyn/dot_general | solution.py:200
  854.7 20.3 %all-to-all-done.11 = f32[8,2,128,512]{2,3,1,0:T(8,128)} async-done(((f32[8,2,128,512]{2,3,1,0:T(8,128)}), f32[8,2,128,512]{2,3,1,0:T(8,128)}, u32[]{:S(2)}, u32[]{:S(2)}) %all-to-all-start.11) | async-done | bytes 4194336 | tf_op jit(solution)/shard_map/all_to_all | solution.py:198
  885.4 19.3 %fusion.62 = bf16[2,128,2048]{2,1,0:T(8,128)(2,1)} fusion(f32[2,128,4096]{2,1,0:T(8,128)} %reshape.326, f32[2048,4096]{1,0:T(8,128)} %bitcast.277), kind=kOutput, calls=%fused_computation.71 | convolution fusion | flops 12885950464 | bytes 38797312 | tf_op jit(solution)/shard_map/zyc,nc->zyn/dot_general | solution.py:200
  (114 shorter events, 291.2 us)
Async XLA Ops:
  1.1 20.1 %collective-permute-start = (bf16[1,128,2048]{2,1,0:T(8,128)(2,1)S(1)}, bf16[1,128,2048]{2,1,0:T(8,128)(2,1)S(1)}, u32[]{:S(2)}, u32[]{:S(2)}) collective-permute-start(bf16[1,128,2048]{2,1,0:T(8,128)(2,1)S(1)} %slice.103), channel_id=1, source_target_pairs={{1,0},{2,1},{3,2},{5,4},{6,5},{7,6},{9,8},{10,9},{11,10},{13,12},{... | collective-permute-start | bytes 1572872 | tf_op jit(solution)/shard_map/ppermute | solution.py:17
  8.6 11.6 %copy-start = (bf16[8,128,2048]{2,1,0:T(8,128)(2,1)S(1)}, bf16[8,128,2048]{2,1,0:T(8,128)(2,1)}, u32[]{:S(2)}) copy-start(bf16[8,128,2048]{2,1,0:T(8,128)(2,1)} %param.7) | copy-start | bytes 12582916
  52.3 54.4 %all-to-all-start.1 = ((f32[8,2,128,512]{3,2,1,0:T(8,128)}), f32[8,2,128,512]{3,2,1,0:T(8,128)}, u32[]{:S(2)}, u32[]{:S(2)}) async-start(f32[8,2,128,512]{3,2,1,0:T(8,128)} %bitcast.281), calls=%async_computation.1 | async-start | bytes 8388608 | tf_op jit(solution)/shard_map/all_to_all | solution.py:146
  106.7 65.2 %all-to-all-start = ((f32[8,2,128,512]{3,2,1,0:T(8,128)}), f32[8,2,128,512]{3,2,1,0:T(8,128)}, u32[]{:S(2)}, u32[]{:S(2)}) async-start(f32[8,2,128,512]{3,2,1,0:T(8,128)} %bitcast.278), calls=%async_computation | async-start | bytes 8388608 | tf_op jit(solution)/shard_map/all_to_all | solution.py:146
  152.3 11.3 %copy-start.5 = (f32[32,32,1024]{2,1,0:T(8,128)S(1)}, f32[32,32,1024]{2,1,0:T(8,128)}, u32[]{:S(2)}) copy-start(f32[32,32,1024]{2,1,0:T(8,128)} %get-tuple-element.78) | copy-start | bytes 12582916
  152.3 11.3 %copy-start.9 = (f32[2,512,1024]{2,1,0:T(8,128)S(1)}, f32[2,512,1024]{2,1,0:T(8,128)}, u32[]{:S(2)}) copy-start(f32[2,512,1024]{2,1,0:T(8,128)} %copy.32) | copy-start | bytes 12582916
  171.9 60.2 %all-to-all-start.3 = ((f32[8,2,128,512]{3,2,1,0:T(8,128)}), f32[8,2,128,512]{3,2,1,0:T(8,128)}, u32[]{:S(2)}, u32[]{:S(2)}) async-start(f32[8,2,128,512]{3,2,1,0:T(8,128)} %bitcast.279), calls=%async_computation.3 | async-start | bytes 8388608 | tf_op jit(solution)/shard_map/all_to_all | solution.py:146
  212.5 11.3 %copy-start.6 = (f32[32,32,1024]{2,1,0:T(8,128)S(1)}, f32[32,32,1024]{2,1,0:T(8,128)}, u32[]{:S(2)}) copy-start(f32[32,32,1024]{2,1,0:T(8,128)} %get-tuple-element.78) | copy-start | bytes 12582916
  212.5 11.3 %copy-start.10 = (f32[2,512,1024]{2,1,0:T(8,128)S(1)}, f32[2,512,1024]{2,1,0:T(8,128)}, u32[]{:S(2)}) copy-start(f32[2,512,1024]{2,1,0:T(8,128)} %copy.28) | copy-start | bytes 12582916
  232.1 54.1 %all-to-all-start.2 = ((f32[8,2,128,512]{3,2,1,0:T(8,128)}), f32[8,2,128,512]{3,2,1,0:T(8,128)}, u32[]{:S(2)}, u32[]{:S(2)}) async-start(f32[8,2,128,512]{3,2,1,0:T(8,128)} %bitcast.280), calls=%async_computation.2 | async-start | bytes 8388608 | tf_op jit(solution)/shard_map/all_to_all | solution.py:146
  247.3 11.3 %copy-start.7 = (f32[32,32,1024]{2,1,0:T(8,128)S(1)}, f32[32,32,1024]{2,1,0:T(8,128)}, u32[]{:S(2)}) copy-start(f32[32,32,1024]{2,1,0:T(8,128)} %get-tuple-element.78) | copy-start | bytes 12582916
  247.3 11.3 %copy-start.11 = (f32[2,512,1024]{2,1,0:T(8,128)S(1)}, f32[2,512,1024]{2,1,0:T(8,128)}, u32[]{:S(2)}) copy-start(f32[2,512,1024]{2,1,0:T(8,128)} %copy.36) | copy-start | bytes 12582916
  296.5 11.3 %copy-start.8 = (f32[32,32,1024]{2,1,0:T(8,128)S(1)}, f32[32,32,1024]{2,1,0:T(8,128)}, u32[]{:S(2)}) copy-start(f32[32,32,1024]{2,1,0:T(8,128)} %get-tuple-element.78) | copy-start | bytes 12582916
  296.5 11.3 %copy-start.12 = (f32[2,512,1024]{2,1,0:T(8,128)S(1)}, f32[2,512,1024]{2,1,0:T(8,128)}, u32[]{:S(2)}) copy-start(f32[2,512,1024]{2,1,0:T(8,128)} %copy.34) | copy-start | bytes 12582916
  654.5 56.3 %all-to-all-start.8 = ((f32[8,2,128,512]{2,3,1,0:T(8,128)}), f32[8,2,128,512]{2,3,1,0:T(8,128)}, u32[]{:S(2)}, u32[]{:S(2)}) async-start(f32[8,2,128,512]{2,3,1,0:T(8,128)} %bitcast_bitcast_fusion.2), calls=%async_computation.8 | async-start | bytes 8388608 | tf_op jit(solution)/shard_map/all_to_all | solution.py:198
  661.7 10.6 %copy-start.2 = (f32[32,32,1024]{2,1,0:T(8,128)S(1)}, f32[32,32,1024]{2,1,0:T(8,128)}, u32[]{:S(2)}) copy-start(f32[32,32,1024]{2,1,0:T(8,128)} %get-tuple-element.77) | copy-start | bytes 12582916
  661.7 10.6 %copy-start.17 = (f32[2,2,256,1024]{3,2,1,0:T(8,128)S(1)}, f32[2,2,256,1024]{3,2,1,0:T(8,128)}, u32[]{:S(2)}) copy-start(f32[2,2,256,1024]{3,2,1,0:T(8,128)} %get-tuple-element.53) | copy-start | bytes 12582916
  710.8 55.4 %all-to-all-start.9 = ((f32[8,2,128,512]{2,3,1,0:T(8,128)}), f32[8,2,128,512]{2,3,1,0:T(8,128)}, u32[]{:S(2)}, u32[]{:S(2)}) async-start(f32[8,2,128,512]{2,3,1,0:T(8,128)} %bitcast_bitcast_fusion), calls=%async_computation.9 | async-start | bytes 8388608 | tf_op jit(solution)/shard_map/all_to_all | solution.py:198
  715.9 10.6 %copy-start.3 = (f32[32,32,1024]{2,1,0:T(8,128)S(1)}, f32[32,32,1024]{2,1,0:T(8,128)}, u32[]{:S(2)}) copy-start(f32[32,32,1024]{2,1,0:T(8,128)} %get-tuple-element.77) | copy-start | bytes 12582916
  715.9 10.6 %copy-start.16 = (f32[2,2,256,1024]{3,2,1,0:T(8,128)S(1)}, f32[2,2,256,1024]{3,2,1,0:T(8,128)}, u32[]{:S(2)}) copy-start(f32[2,2,256,1024]{3,2,1,0:T(8,128)} %get-tuple-element.49) | copy-start | bytes 12582916
  766.3 54.9 %all-to-all-start.10 = ((f32[8,2,128,512]{2,3,1,0:T(8,128)}), f32[8,2,128,512]{2,3,1,0:T(8,128)}, u32[]{:S(2)}, u32[]{:S(2)}) async-start(f32[8,2,128,512]{2,3,1,0:T(8,128)} %bitcast_bitcast_fusion.3), calls=%async_computation.10 | async-start | bytes 8388608 | tf_op jit(solution)/shard_map/all_to_all | solution.py:198
  770.9 10.6 %copy-start.4 = (f32[32,32,1024]{2,1,0:T(8,128)S(1)}, f32[32,32,1024]{2,1,0:T(8,128)}, u32[]{:S(2)}) copy-start(f32[32,32,1024]{2,1,0:T(8,128)} %get-tuple-element.77) | copy-start | bytes 12582916
  770.9 10.6 %copy-start.15 = (f32[2,2,256,1024]{3,2,1,0:T(8,128)S(1)}, f32[2,2,256,1024]{3,2,1,0:T(8,128)}, u32[]{:S(2)}) copy-start(f32[2,2,256,1024]{3,2,1,0:T(8,128)} %get-tuple-element.52) | copy-start | bytes 12582916
  821.2 53.7 %all-to-all-start.11 = ((f32[8,2,128,512]{2,3,1,0:T(8,128)}), f32[8,2,128,512]{2,3,1,0:T(8,128)}, u32[]{:S(2)}, u32[]{:S(2)}) async-start(f32[8,2,128,512]{2,3,1,0:T(8,128)} %bitcast_bitcast_fusion.1), calls=%async_computation.11 | async-start | bytes 8388608 | tf_op jit(solution)/shard_map/all_to_all | solution.py:198
  (4 other events, 25.6 us)
